TPU v7x, 32 devices: a whole 2x2x4 slice. The times are simulated.
32 devices in a mesh: groups: 2 (over y), ctx: 4 (over z), exp: 4 (over x, core), rep: 1.
Axes of the slice: x: 2, y: 2, z: 4, core: 2. Of those that a mesh axis runs over, the one named last changes fastest.
Arguments:
- queries: bfloat16 [2, 256, 4096], P('groups', 'ctx', ('exp', 'rep')), parts along dimension 0, may hold values from -16.25 to 16.25
- pages: bfloat16 [2, 2304, 2, 512], P('groups', 'ctx', None, 'exp'), parts along dimension 0, may hold values from -5.2 to 5.2
- cached_lengths: int32 [2, 4], P('groups'), parts along dimension 0, may hold values from 128 to 512
- residual_in: bfloat16 [2, 256, 2048], P('groups', ('ctx', 'exp')), parts along dimension 0, may hold values from -2.390625 to 2.390625
- out_weight: bfloat16 [4096, 2048], P(('exp', 'rep')), may hold values from -0.09375 to 0.09375
- norm_gain: float32 [2048], replicated, may hold values from 0.1 to 1.9
- expert_ids: int32 [2, 256, 8], P('groups', ('ctx', 'exp')), parts along dimension 0, may hold values from 0 to 15, all different within a row; in each aligned block of 16 rows (0 to 15, 16 to 31, ..., all dimensions but the last counted through in order) at most 8 rows name the same one
- route_scores: float32 [2, 256, 8], P('groups', ('ctx', 'exp')), parts along dimension 0, may hold values from 0.05 to 1
- expert_input: bfloat16 [16, 2048, 2, 384], P(('ctx', 'exp'), None, None, 'rep'), may hold values from -0.125 to 0.125
- expert_output: bfloat16 [16, 384, 2048], P(('ctx', 'exp'), 'rep'), may hold values from -0.3125 to 0.3125
Outputs:
- context: bfloat16 [2, 256, 4096], P('groups', 'ctx', ('exp', 'rep')), parts along dimension 0
- layer_out: bfloat16 [2, 256, 2048], P('groups', ('ctx', 'exp', 'rep')), parts along dimension 0
There are 2 independent parts, one for each index of `groups`. A program takes and returns all parts, laid end to end along the dimension named above; an argument that names none is the same for every part. Nothing has to cross between parts.
Inputs may be any that keep to these rules, and one draw needn't show every extreme that they name: `expert_ids`: in every aligned block of 16 positions of one request, no expert is named by more than 8 of the block's rows, and in some blocks one expert by exactly 8; the 8 experts of a row differ.
All inputs are finite; a program needn't handle non-finite values.
Results may differ from a plain program's by a relative error of at most 0.015.
Values may be sent and summed in bfloat16 or wider, within the bound.
A program may use at most 128 MiB of HBM per device.

v0:
```python
import jax
import jax.numpy as jnp
from jax import lax
from jax.sharding import PartitionSpec as P

HEAD = 128
floor_value = -1e30
norm_epsilon = 1e-06


def normalize(hidden, norm_gain):
    widened = hidden.astype(jnp.float32)
    mean_square = jnp.mean(widened * widened, axis=-1, keepdims=True)
    return (widened * lax.rsqrt(mean_square + norm_epsilon) * norm_gain).astype(jnp.bfloat16)


def attend_piece(query_rows, page_rows, allowed):
    scaling = query_rows.shape[-1] ** (-0.5)
    scores = (
        jnp.einsum(
            "rqhe,rke->rqhk", query_rows, page_rows[:, :, 0], preferred_element_type=jnp.float32
        )
        * scaling
    )
    permitted = allowed[:, :, None, :]
    masked = jnp.where(permitted, scores, floor_value)
    peaks = jnp.max(masked, axis=-1)
    weights = jnp.where(permitted, jnp.exp(masked - peaks[..., None]), 0.0)
    totals = jnp.sum(weights, axis=-1)
    summed = jnp.einsum(
        "rqhk,rke->rqhe",
        weights.astype(jnp.bfloat16),
        page_rows[:, :, 1],
        preferred_element_type=jnp.float32,
    )
    return (peaks, totals, summed)


def merge_partials(earlier, later):
    peaks = jnp.maximum(earlier[0], later[0])
    later_scale = jnp.exp(later[0] - peaks)
    totals = later[1] * later_scale
    summed = later[2] * later_scale[..., None]
    return (peaks, totals, summed)


def rows_mask(row_index, lengths, query_positions, slab_size, fresh_block):
    page_size = slab_size + fresh_block
    page_number = row_index // page_size
    offset = row_index - page_number * page_size
    page_count = lengths.shape[1]
    picker = page_number[None, :] == jnp.arange(page_count, dtype=jnp.int32)[:, None]
    live_length = jnp.sum(jnp.where(picker[None], lengths[:, :, None], 0), axis=1)
    in_cache = (offset < slab_size)[None, :] & (offset[None, :] < live_length)
    fresh_position = page_number * fresh_block + offset - slab_size
    in_fresh = (offset >= slab_size)[None, :] & (
        fresh_position[None, :] <= query_positions[:, None]
    )
    return in_cache[:, None, :] | in_fresh[None, :, :]


def per_device(
    queries,
    pages,
    cached_lengths,
    residual_in,
    out_weight,
    norm_gain,
    expert_ids,
    route_scores,
    expert_input,
    expert_output,
):
    requests, fresh_block, query_width = queries.shape
    local_heads = query_width // HEAD
    core_place = lax.axis_index("rep")
    page_place = lax.axis_index("ctx")
    rep_count = lax.axis_size("rep")
    page_size = pages.shape[1]
    slab_size = page_size - fresh_block
    own_positions = page_place * fresh_block + jnp.arange(fresh_block, dtype=jnp.int32)
    query_rows = queries.reshape(requests, fresh_block, local_heads, HEAD)
    start_state = (
        jnp.full((requests, fresh_block, local_heads), floor_value, jnp.float32),
        jnp.zeros((requests, fresh_block, local_heads), jnp.float32),
        jnp.zeros((requests, fresh_block, local_heads, HEAD), jnp.float32),
    )
    page_piece = lax.all_gather(pages, "ctx", axis=1, tiled=True)
    row_index = jnp.arange(page_piece.shape[1], dtype=jnp.int32)
    allowed = rows_mask(row_index, cached_lengths, own_positions, slab_size, fresh_block)
    peaks, totals, summed = merge_partials(
        start_state, attend_piece(query_rows, page_piece, allowed)
    )
    context = (
        (summed / totals[..., None])
        .astype(jnp.bfloat16)
        .reshape(requests, fresh_block, query_width)
    )
    projected = jnp.dot(
        context.reshape(requests * fresh_block, query_width),
        out_weight,
        preferred_element_type=jnp.float32,
    ).reshape(requests, fresh_block, -1)
    token_block = residual_in.shape[1]
    share_size = token_block // rep_count
    own_share = lax.psum_scatter(
        projected.astype(jnp.bfloat16), ("exp", "rep"), scatter_dimension=1, tiled=True
    ).astype(jnp.float32)
    own_residual = lax.dynamic_slice_in_dim(residual_in, core_place * share_size, share_size, 1)
    own_hidden = (own_residual.astype(jnp.float32) + own_share).astype(jnp.bfloat16)
    normed = lax.all_gather(normalize(own_hidden, norm_gain), "rep", axis=1, tiled=True)
    top_count = expert_ids.shape[2]
    expert_count = lax.axis_size("ctx") * lax.axis_size("exp")
    most_rows = max(2, (token_block * top_count + expert_count - 1) // expert_count)
    capacity = requests * most_rows
    model_width = normed.shape[2]
    token_count = requests * token_block
    flat_ids = expert_ids.reshape(-1)
    row_count = flat_ids.shape[0]
    chosen = (flat_ids[:, None] == jnp.arange(expert_count, dtype=jnp.int32)[None, :]).astype(
        jnp.int32
    )
    earlier_rows = jnp.cumsum(chosen, axis=0) - chosen
    slot_rank = jnp.sum(earlier_rows * chosen, axis=1)
    slot_index = flat_ids * capacity + slot_rank
    slot_onehot = (
        slot_index[:, None] == jnp.arange(expert_count * capacity, dtype=jnp.int32)[None, :]
    ).astype(jnp.bfloat16)
    token_onehot = (
        (jnp.arange(row_count, dtype=jnp.int32) // top_count)[:, None]
        == jnp.arange(token_count, dtype=jnp.int32)[None, :]
    ).astype(jnp.bfloat16)
    placement = jnp.dot(slot_onehot.T, token_onehot, preferred_element_type=jnp.float32).astype(
        jnp.bfloat16
    )
    outgoing = jnp.dot(
        placement, normed.reshape(token_count, model_width), preferred_element_type=jnp.float32
    )
    outgoing = outgoing.astype(jnp.bfloat16).reshape(expert_count, capacity, model_width)
    scores_sum = jnp.sum(route_scores, axis=2, keepdims=True)
    combine = (route_scores / scores_sum).astype(jnp.bfloat16).reshape(-1)
    gathering = jnp.dot(
        (token_onehot * combine[:, None]).T, slot_onehot, preferred_element_type=jnp.float32
    ).astype(jnp.bfloat16)
    gate_up = expert_input[0]
    down_weight = expert_output[0]
    arrived_rows = lax.all_to_all(outgoing, ("ctx", "exp"), split_axis=0, concat_axis=0, tiled=True)
    inner_rows = jnp.einsum(
        "nd,dgh->ngh",
        arrived_rows.reshape(-1, model_width),
        gate_up,
        preferred_element_type=jnp.float32,
    )
    activated = (jax.nn.silu(inner_rows[:, 0]) * inner_rows[:, 1]).astype(jnp.bfloat16)
    result = jnp.dot(activated, down_weight, preferred_element_type=jnp.float32).astype(
        jnp.bfloat16
    )
    returned = lax.all_to_all(
        result.reshape(arrived_rows.shape), ("ctx", "exp"), split_axis=0, concat_axis=0, tiled=True
    )
    mixture = jnp.dot(
        gathering,
        returned.reshape(expert_count * capacity, model_width),
        preferred_element_type=jnp.float32,
    )
    own_mixture = lax.psum_scatter(
        mixture.reshape(requests, token_block, model_width).astype(jnp.bfloat16),
        "rep",
        scatter_dimension=1,
        tiled=True,
    ).astype(jnp.float32)
    layer_out = (own_hidden.astype(jnp.float32) + own_mixture).astype(jnp.bfloat16)
    return (context, layer_out)


def solution(mesh):
    in_specs = (
        P("groups", "ctx", ("exp", "rep")),
        P("groups", "ctx", None, "exp"),
        P("groups", None),
        P("groups", ("ctx", "exp"), None),
        P(("exp", "rep"), None),
        P(),
        P("groups", ("ctx", "exp"), None),
        P("groups", ("ctx", "exp"), None),
        P(("ctx", "exp"), None, None, "rep"),
        P(("ctx", "exp"), "rep", None),
    )
    out_specs = (P("groups", "ctx", ("exp", "rep")), P("groups", ("ctx", "exp", "rep"), None))
    return jax.shard_map(
        per_device, mesh=mesh, in_specs=in_specs, out_specs=out_specs, check_vma=False
    )
```

profile of v0, /device:TPU:0, one launch (start us, length us, event | category | flops | bytes accessed | tf_op | source)
XLA Modules:
  0.0 121.3 jit_solution(10408529155012849360)
XLA Ops:
  7.2 0.0 copy-start
  7.2 0.0 all-gather.2.cloned.1.call-start
  7.2 1.9 %copy.20 = bf16[1,576,2,128]{3,1,2,0:T(8,128)(2,1)} copy(bf16[1,576,2,128]{3,2,1,0:T(2,128)(2,1)} %param.11) | data formatting | bytes 589824 | tf_op args[1]
  9.1 0.0 all-gather.2.cloned.1.call-update
  9.1 0.0 reduce-scatter.2.cloned.1.call-start
  9.2 0.9 copy.24
  10.1 0.8 copy.22
  10.9 0.1 reshape.327
  11.0 0.8 select_reduce_fusion.1
  11.8 0.2 and_or_fusion
  12.0 30.6 %all-gather.2.cloned.1.call-done = bf16[1,2304,2,128]{3,1,2,0:T(8,128)(2,1)} async-done(((bf16[1,576,2,128]{3,1,2,0:T(8,128)(2,1)}), bf16[1,2304,2,128]{3,1,2,0:T(8,128)(2,1)}) %all-gather.2.cloned.1.call-update) | async-done | bytes 1179664 | tf_op jit(solution)/shard_map/all_gather | solution.py:88
  42.6 2.5 %fusion.70 = (f32[64,8]{1,0:T(8,128)S(1)}, f32[64,8,2304]{2,1,0:T(8,128)S(1)}) fusion(bf16[64,8,128]{2,1,0:T(8,128)(2,1)S(1)} %bitcast.57, bf16[1,2304,2,128]{3,1,2,0:T(8,128)(2,1)} %all-gather.2.cloned.1.call-done, pred[64,2304]{1,0:T(8,128)(4,1)S(1)} %and_or_fusion), kind=kOutput, calls=%fused_computation.88 | convolution fusion | flops 305528320 | bytes 5588992 | tf_op jit(solution)/shard_map/rqhe,rke->rqhk/dot_general | solution.py:20
  45.1 1.3 %fusion.1 = f32[64,8]{1,0:T(8,128)S(1)} fusion(f32[64,8,2304]{2,1,0:T(8,128)S(1)} %get-tuple-element.5, f32[64,8]{1,0:T(8,128)S(1)} %get-tuple-element.4, pred[64,2304]{1,0:T(8,128)(4,1)S(1)} %and_or_fusion), kind=kLoop, calls=%fused_computation.3 | loop fusion | flops 3538432 | bytes 4870144 | tf_op jit(solution)/shard_map/reduce_sum | solution.py:29
  46.4 1.1 fusion.24
  47.5 1.0 copy-done.1
  48.5 1.5 %fusion.12 = bf16[1,64,2048]{2,1,0:T(8,128)(2,1)} fusion(bf16[1024,2048]{1,0:T(8,128)(2,1)S(1)} %copy-done.1, bf16[8,8,8,128]{3,2,1,0:T(8,128)(2,1)S(1)} %bitcast.56), kind=kOutput, calls=%fused_computation.16 | convolution fusion | flops 268566528 | bytes 4587520 | tf_op jit(solution)/shard_map/dot_general | solution.py:99
  50.1 0.0 reduce-scatter.2.cloned.1.call-update
  50.1 0.1 fusion.41
  50.2 0.2 reduce_window_sum.11
  50.4 0.2 select_reduce_fusion
  50.6 19.0 %reduce-scatter.2.cloned.1.call-done = bf16[1,16,2048]{2,1,0:T(8,128)(2,1)} async-done(((bf16[1,64,2048]{2,1,0:T(8,128)(2,1)}), bf16[1,16,2048]{2,1,0:T(8,128)(2,1)}) %reduce-scatter.2.cloned.1.call-update) | async-done | bytes 65552 | tf_op jit(solution)/shard_map/reduce_scatter | solution.py:106
  69.6 1.0 fusion.30
  70.6 2.2 %fusion.10 = bf16[16,8,2048]{2,1,0:T(8,128)(2,1)} fusion(f32[2048]{0:T(1024)S(1)} %copy-done.7, f32[16]{0:T(128)S(1)} %add_rsqrt_fusion, s32[128]{0:T(128)S(1)} %get-tuple-element.9, s32[128]{0:T(128)S(1)} %get-tuple-element.8, bf16[1,16,2048]{2,1,0:T(8,128)(2,1)} %reduce-scatter.2.cloned.1.call-done, bf16[1,16,2048]{2,1,0:T(8,128)(2,1)S(1)} %copy-done.3), kind=kOutput, calls=%fused_computation.13 | convolution fusion | flops 9457664 | bytes 664640 | tf_op jit(solution)/shard_map/dot_general | solution.py:136
  72.8 19.1 %all_to_all.10 = bf16[16,8,2048]{2,1,0:T(8,128)(2,1)S(1)} all-to-all(bf16[16,8,2048]{2,1,0:T(8,128)(2,1)} %fusion.10), channel_id=1, replica_groups=mesh['groups'=2,'ctx'=4,'exp'=4,'rep'=1] {'ctx','exp'}, dimensions={0} | all-to-all | bytes 1048576 | tf_op jit(solution)/shard_map/all_to_all | solution.py:147
  91.9 0.6 fusion.3
  92.5 1.3 %fusion.11 = bf16[16,8,2048]{2,1,0:T(8,128)(2,1)} fusion(bf16[1,384,2048]{2,1,0:T(8,128)(2,1)S(1)} %copy-done.2, f32[128,2,384]{2,0,1:T(8,128)S(1)} %fusion.3), kind=kOutput, calls=%fused_computation.14 | convolution fusion | flops 201883648 | bytes 2490368 | tf_op jit(solution)/shard_map/dot_general | solution.py:155
  93.8 4.2 %all-to-all-start.1 = ((bf16[16,8,2048]{2,1,0:T(8,128)(2,1)}), bf16[16,8,2048]{2,1,0:T(8,128)(2,1)}, u32[]{:S(2)}, u32[]{:S(2)}) async-start(bf16[16,8,2048]{2,1,0:T(8,128)(2,1)} %fusion.11), calls=%async_computation.2 | async-start | bytes 1048576 | tf_op jit(solution)/shard_map/all_to_all | solution.py:158
  98.1 0.1 copy.21
  98.2 0.1 mul.119
  98.3 0.7 reshape.326
  99.0 13.4 %all-to-all-done.1 = bf16[16,8,2048]{2,1,0:T(8,128)(2,1)} async-done(((bf16[16,8,2048]{2,1,0:T(8,128)(2,1)}), bf16[16,8,2048]{2,1,0:T(8,128)(2,1)}, u32[]{:S(2)}, u32[]{:S(2)}) %all-to-all-start.1) | async-done | bytes 524320 | tf_op jit(solution)/shard_map/all_to_all | solution.py:158
  112.4 2.1 %fusion.16 = bf16[1,16,2048]{2,1,0:T(8,128)(2,1)} fusion(bf16[16,8,2048]{2,1,0:T(8,128)(2,1)} %all-to-all-done.1, s32[128]{0:T(128)S(1)} %get-tuple-element.9, s32[128]{0:T(128)S(1)} %get-tuple-element.8, bf16[128]{0:T(256)(128)(2,1)S(1)} %mul.119, bf16[1,16,2048]{2,1,0:T(8,128)(2,1)S(1)} %copy-done.4, bf16[1,16,2048]{2,1,0:T(8,128)(2,1)S(1)} %copy-done.3), kind=kOutput, calls=%fused_computation.21 | convolution fusion | flops 9230336 | bytes 722176 | tf_op jit(solution)/shard_map/dot_general | solution.py:161
  (23 shorter events, 0.1 us)
Async XLA Ops:
  7.2 84.7 %copy-start = (bf16[1,2048,2,384]{3,2,1,0:T(2,128)(2,1)S(1)}, bf16[1,2048,2,384]{3,2,1,0:T(2,128)(2,1)}, u32[]{:S(2)}) copy-start(bf16[1,2048,2,384]{3,2,1,0:T(2,128)(2,1)} %param.18) | copy-start | bytes 9437188
  7.2 35.4 %all-gather.2.cloned.1.call-start = ((), (), s32[]{:S(2)}) async-start(), calls=%async_computation.3 | async-start | bytes 1474560 | tf_op jit(solution)/shard_map/all_gather | solution.py:88
  9.1 60.5 %reduce-scatter.2.cloned.1.call-start = ((), (), s32[]{:S(2)}) async-start(), calls=%async_computation.4 | async-start | bytes 327680 | tf_op jit(solution)/shard_map/reduce_scatter | solution.py:106
  42.6 3.8 %copy-start.5 = (bf16[1,2304,2,128]{3,1,2,0:T(8,128)(2,1)S(1)}, bf16[1,2304,2,128]{3,1,2,0:T(8,128)(2,1)}, u32[]{:S(2)}) copy-start(bf16[1,2304,2,128]{3,1,2,0:T(8,128)(2,1)} %all-gather.2.cloned.1.call-done) | copy-start | bytes 3538948
  46.4 2.2 %copy-start.1 = (bf16[1024,2048]{1,0:T(8,128)(2,1)S(1)}, bf16[1024,2048]{1,0:T(8,128)(2,1)}, u32[]{:S(2)}) copy-start(bf16[1024,2048]{1,0:T(8,128)(2,1)} %param.14) | copy-start | bytes 12582916
  47.5 22.1 %copy-start.3 = (bf16[1,16,2048]{2,1,0:T(8,128)(2,1)S(1)}, bf16[1,16,2048]{2,1,0:T(8,128)(2,1)}, u32[]{:S(2)}) copy-start(bf16[1,16,2048]{2,1,0:T(8,128)(2,1)} %param.13) | copy-start | bytes 196612
  47.5 23.1 %copy-start.7 = (f32[2048]{0:T(1024)S(1)}, f32[2048]{0:T(1024)}, u32[]{:S(2)}) copy-start(f32[2048]{0:T(1024)} %param.15) | copy-start | bytes 24580
  72.8 19.8 %copy-start.2 = (bf16[1,384,2048]{2,1,0:T(8,128)(2,1)S(1)}, bf16[1,384,2048]{2,1,0:T(8,128)(2,1)}, u32[]{:S(2)}) copy-start(bf16[1,384,2048]{2,1,0:T(8,128)(2,1)} %param.19) | copy-start | bytes 4718596
  91.9 6.2 %copy-start.6 = (f32[1,16,8]{1,2,0:T(8,128)S(1)}, f32[1,16,8]{1,2,0:T(8,128)}, u32[]{:S(2)}) copy-start(f32[1,16,8]{1,2,0:T(8,128)} %param.17) | copy-start | bytes 1540
  91.9 20.5 %copy-start.4 = (bf16[1,16,2048]{2,1,0:T(8,128)(2,1)S(1)}, bf16[1,16,2048]{2,1,0:T(8,128)(2,1)}, u32[]{:S(2)}) copy-start(bf16[1,16,2048]{2,1,0:T(8,128)(2,1)} %reduce-scatter.2.cloned.1.call-done) | copy-start | bytes 196612
  93.8 18.6 %all-to-all-start.1 = ((bf16[16,8,2048]{2,1,0:T(8,128)(2,1)}), bf16[16,8,2048]{2,1,0:T(8,128)(2,1)}, u32[]{:S(2)}, u32[]{:S(2)}) async-start(bf16[16,8,2048]{2,1,0:T(8,128)(2,1)} %fusion.11), calls=%async_computation.2 | async-start | bytes 1048576 | tf_op jit(solution)/shard_map/all_to_all | solution.py:158
Sparse Core Ops, SparseCore 0:
  9.6 32.9 all-gather.1
  50.2 19.2 reduce-scatter.1
where the time goes:
time: 122 us; the launch traced here: 121 us
  waiting for transfers between devices  63 us (52%)
  blocking collectives  19.1 us (16%)
  between operations  14.2 us (12%)
  matrix products  11.3 us (9%)
  local copies, waits for them, and re-layouts  5.62 us (5%)
  starting transfers between devices  4.32 us (4%)
  other arithmetic  3.74 us (3%)
    all_gather x1, waiting for transfers between devices, per_device(): page_piece = lax.all_gather(pages, 'ctx', axis=1, tiled=True)  30.6 us
    all_to_all x1, blocking collectives, per_device(): lax.all_to_all(outgoing, ('ctx', 'exp'), split_axis=0, concat_axis=0, til...  19.1 us
    reduce_scatter x1, waiting for transfers between devices, per_device(): lax.psum_scatter(projected.astype(jnp.bfloat16), ('exp', 'rep'), scatter_...  19 us
    all_to_all x1, waiting for transfers between devices, per_device(): lax.all_to_all(result.reshape(arrived_rows.shape), ('ctx', 'exp'), split_...  13.4 us
    unnamed x19, local copies, waits for them, and re-layouts  4.63 us
    all_to_all x1, starting transfers between devices, per_device(): lax.all_to_all(result.reshape(arrived_rows.shape), ('ctx', 'exp'), split_...  4.24 us
    dot_general x1, matrix products, attend_piece(): jnp.einsum('rqhe,rke->rqhk', query_rows, page_rows[:, :, 0], preferred_el...  2.46 us
  transfers between devices with their start and end apart: 3, of which 3 were waited for; matrix products, arithmetic and copies ran while one was open for 3% of the time, Pallas kernels for 0%

commit v1 on v0

--- a/solution.py
+++ b/solution.py
@@ -85,7 +85,14 @@
         jnp.zeros((requests, fresh_block, local_heads), jnp.float32),
         jnp.zeros((requests, fresh_block, local_heads, HEAD), jnp.float32),
     )
-    page_piece = lax.all_gather(pages, "ctx", axis=1, tiled=True)
+    ways, here = (lax.axis_size("ctx"), lax.axis_index("ctx"))
+    page_piece, reach = (pages, 1)
+    while reach < ways:
+        theirs = lax.ppermute(page_piece, "ctx", [(d, d ^ reach) for d in range(ways)])
+        mine_first = jnp.concatenate([page_piece, theirs], axis=1)
+        theirs_first = jnp.concatenate([theirs, page_piece], axis=1)
+        page_piece = jnp.where(here & reach == 0, mine_first, theirs_first)
+        reach = 2 * reach
     row_index = jnp.arange(page_piece.shape[1], dtype=jnp.int32)
     allowed = rows_mask(row_index, cached_lengths, own_positions, slab_size, fresh_block)
     peaks, totals, summed = merge_partials(

time: 122 us -> 128 us (1.049)
  starting transfers between devices: 4.32 us -> 10.2 us
  other arithmetic: 3.74 us -> 6.27 us
  matrix products: 11.3 us -> 9.73 us
    all_gather x1 -> x0, waiting for transfers between devices: 30.6 us -> none  [per_device(): page_piece = lax.all_gather(pages, 'ctx', axis=1, tiled=True)]
    ppermute x0 -> x2, waiting for transfers between devices: none -> 27.7 us  [per_device(): lax.ppermute(page_piece, 'ctx', [(d, d ^ reach) for d in range(ways)])]
    ppermute x0 -> x2, starting transfers between devices: none -> 5.93 us  [per_device(): lax.ppermute(page_piece, 'ctx', [(d, d ^ reach) for d in range(ways)])]
    reduce_scatter x1, waiting for transfers between devices: 19 us -> 20.8 us  [per_device(): lax.psum_scatter(projected.astype(jnp.bfloat16), ('exp', 'rep'), scatter_...]
    select_n x0 -> x2, other arithmetic: none -> 1.51 us  [per_device(): page_piece = jnp.where(here & reach == 0, mine_first, theirs_first)]
    dot_general x1, matrix products: 2.46 us -> 1.08 us  [attend_piece(): jnp.einsum('rqhe,rke->rqhk', query_rows, page_rows[:, :, 0], preferred_el...]
  transfers between devices with their start and end apart: 3 -> 4, of which waited for: 3 -> 4; matrix products, arithmetic and copies ran while one was open for 3% -> 5% of each run, Pallas kernels for 0% -> 0%
where the time goes in v1:
time: 128 us
  waiting for transfers between devices  61.8 us (48%)
  blocking collectives  19 us (15%)
  between operations  14.2 us (11%)
  starting transfers between devices  10.2 us (8%)
  matrix products  9.73 us (8%)
  local copies, waits for them, and re-layouts  6.68 us (5%)
  other arithmetic  6.27 us (5%)
    ppermute x2, waiting for transfers between devices, per_device(): lax.ppermute(page_piece, 'ctx', [(d, d ^ reach) for d in range(ways)])  27.7 us
    reduce_scatter x1, waiting for transfers between devices, per_device(): lax.psum_scatter(projected.astype(jnp.bfloat16), ('exp', 'rep'), scatter_...  20.8 us
    all_to_all x1, blocking collectives, per_device(): lax.all_to_all(outgoing, ('ctx', 'exp'), split_axis=0, concat_axis=0, til...  19 us
    all_to_all x1, waiting for transfers between devices, per_device(): lax.all_to_all(result.reshape(arrived_rows.shape), ('ctx', 'exp'), split_...  13.3 us
    ppermute x2, starting transfers between devices, per_device(): lax.ppermute(page_piece, 'ctx', [(d, d ^ reach) for d in range(ways)])  5.93 us
    unnamed x19, local copies, waits for them, and re-layouts  5.6 us
    all_to_all x1, starting transfers between devices, per_device(): lax.all_to_all(result.reshape(arrived_rows.shape), ('ctx', 'exp'), split_...  4.24 us
  transfers between devices with their start and end apart: 4, of which 4 were waited for; matrix products, arithmetic and copies ran while one was open for 5% of the time, Pallas kernels for 0%

profile of v1, /device:TPU:0, one launch (start us, length us, event | category | flops | bytes accessed | tf_op | source)
XLA Modules:
  0.0 127.9 jit_solution(17683285578803037300)
XLA Ops:
  7.2 1.2 copy.66
  8.4 3.1 %collective-permute-start = (bf16[1,576,2,128]{3,1,2,0:T(8,128)(2,1)S(1)}, bf16[1,576,2,128]{3,1,2,0:T(8,128)(2,1)}, u32[]{:S(2)}, u32[]{:S(2)}) collective-permute-start(bf16[1,576,2,128]{3,1,2,0:T(8,128)(2,1)S(1)} %copy.66), channel_id=1, source_target_pairs={{0,4},{4,0},{8,12},{12,8},{1,5},{5,1},{9,13},{13,9},{2,6},{6,2},{1... | collective-permute-start | bytes 884744 | tf_op jit(solution)/shard_map/ppermute | solution.py:91
  11.5 1.6 %copy.53 = bf16[8,8,8,128]{3,2,1,0:T(8,128)(2,1)} copy(bf16[8,8,8,128]{3,1,2,0:T(8,128)(2,1)} %bitcast.69) | data formatting | bytes 262144
  13.1 0.8 copy.50
  14.0 0.8 select_reduce_fusion.1
  14.8 3.8 %collective-permute-done = bf16[1,576,2,128]{3,1,2,0:T(8,128)(2,1)} collective-permute-done((bf16[1,576,2,128]{3,1,2,0:T(8,128)(2,1)S(1)}, bf16[1,576,2,128]{3,1,2,0:T(8,128)(2,1)}, u32[]{:S(2)}, u32[]{:S(2)}) %collective-permute-start) | collective-permute-done | bytes 294944 | tf_op jit(solution)/shard_map/ppermute | solution.py:91
  18.6 1.2 maximum_select_fusion.2
  19.8 2.8 %collective-permute-start.1 = (bf16[1,1152,2,128]{3,1,2,0:T(8,128)(2,1)S(1)}, bf16[1,1152,2,128]{3,1,2,0:T(8,128)(2,1)S(1)}, u32[]{:S(2)}, u32[]{:S(2)}) collective-permute-start(bf16[1,1152,2,128]{3,1,2,0:T(8,128)(2,1)S(1)} %maximum_select_fusion.2), channel_id=1, source_target_pairs={{0,8},{4,12},{8,0},{12,4},{1,9},{5,13},{9,1},{13,5},{2,10},{6,14},... | collective-permute-start | bytes 1769480 | tf_op jit(solution)/shard_map/ppermute | solution.py:91
  22.6 0.2 and_or_fusion
  22.8 1.2 fusion.28
  24.0 23.9 %collective-permute-done.1 = bf16[1,1152,2,128]{3,1,2,0:T(8,128)(2,1)S(1)} collective-permute-done((bf16[1,1152,2,128]{3,1,2,0:T(8,128)(2,1)S(1)}, bf16[1,1152,2,128]{3,1,2,0:T(8,128)(2,1)S(1)}, u32[]{:S(2)}, u32[]{:S(2)}) %collective-permute-start.1) | collective-permute-done | bytes 589856 | tf_op jit(solution)/shard_map/ppermute | solution.py:91
  47.9 0.3 maximum_select_fusion
  48.2 1.1 fusion.73
  49.3 1.1 fusion.2
  50.4 0.9 fusion.25
  51.3 1.3 %copy-done.1 = bf16[1024,2048]{1,0:T(8,128)(2,1)S(1)} copy-done((bf16[1024,2048]{1,0:T(8,128)(2,1)S(1)}, bf16[1024,2048]{1,0:T(8,128)(2,1)}, u32[]{:S(2)}) %copy-start.1) | copy-done | bytes 4194328
  52.6 1.6 %fusion.13 = bf16[1,64,2048]{2,1,0:T(8,128)(2,1)} fusion(bf16[1024,2048]{1,0:T(8,128)(2,1)S(1)} %copy-done.1, bf16[64,8,128]{2,0,1:T(8,128)(2,1)S(1)} %fusion.25), kind=kOutput, calls=%fused_computation.17 | convolution fusion | flops 268566528 | bytes 4587520 | tf_op jit(solution)/shard_map/dot_general | solution.py:106
  54.3 0.2 reduce_window_sum.11
  54.5 0.2 select_reduce_fusion
  54.7 20.8 %reduce-scatter.2.cloned.1.call-done = bf16[1,16,2048]{2,1,0:T(8,128)(2,1)} async-done(((bf16[1,64,2048]{2,1,0:T(8,128)(2,1)}), bf16[1,16,2048]{2,1,0:T(8,128)(2,1)}) %reduce-scatter.2.cloned.1.call-update) | async-done | bytes 65552 | tf_op jit(solution)/shard_map/reduce_scatter | solution.py:113
  75.5 1.0 fusion.32
  76.5 2.2 %fusion.11 = bf16[16,8,2048]{2,1,0:T(8,128)(2,1)} fusion(f32[2048]{0:T(1024)S(1)} %copy-done.7, f32[16]{0:T(128)S(1)} %add_rsqrt_fusion, s32[128]{0:T(128)S(1)} %get-tuple-element.11, s32[128]{0:T(128)S(1)} %get-tuple-element.10, bf16[1,16,2048]{2,1,0:T(8,128)(2,1)} %reduce-scatter.2.cloned.1.call-done, bf16[1,16,2048]{2,1,0:T(8,128)(2,1)S(1)} %copy-done.3), kind=kOutput, calls=%fused_computation.14 | convolution fusion | flops 9457664 | bytes 664640 | tf_op jit(solution)/shard_map/dot_general | solution.py:143
  78.7 19.0 %all_to_all.10 = bf16[16,8,2048]{2,1,0:T(8,128)(2,1)S(1)} all-to-all(bf16[16,8,2048]{2,1,0:T(8,128)(2,1)} %fusion.11), channel_id=1, replica_groups=mesh['groups'=2,'ctx'=4,'exp'=4,'rep'=1] {'ctx','exp'}, dimensions={0} | all-to-all | bytes 1048576 | tf_op jit(solution)/shard_map/all_to_all | solution.py:154
  97.7 0.6 fusion.4
  98.3 0.8 copy-done.2
  99.1 1.3 fusion.12
  100.4 4.2 %all-to-all-start.1 = ((bf16[16,8,2048]{2,1,0:T(8,128)(2,1)}), bf16[16,8,2048]{2,1,0:T(8,128)(2,1)}, u32[]{:S(2)}, u32[]{:S(2)}) async-start(bf16[16,8,2048]{2,1,0:T(8,128)(2,1)} %fusion.12), calls=%async_computation.2 | async-start | bytes 1048576 | tf_op jit(solution)/shard_map/all_to_all | solution.py:165
  104.7 0.1 mul.123
  104.8 0.1 copy.47
  104.9 0.7 reshape.494
  105.6 13.3 %all-to-all-done.1 = bf16[16,8,2048]{2,1,0:T(8,128)(2,1)} async-done(((bf16[16,8,2048]{2,1,0:T(8,128)(2,1)}), bf16[16,8,2048]{2,1,0:T(8,128)(2,1)}, u32[]{:S(2)}, u32[]{:S(2)}) %all-to-all-start.1) | async-done | bytes 524320 | tf_op jit(solution)/shard_map/all_to_all | solution.py:165
  118.9 2.1 %fusion.17 = bf16[1,16,2048]{2,1,0:T(8,128)(2,1)} fusion(bf16[16,8,2048]{2,1,0:T(8,128)(2,1)} %all-to-all-done.1, s32[128]{0:T(128)S(1)} %get-tuple-element.11, s32[128]{0:T(128)S(1)} %get-tuple-element.10, bf16[128]{0:T(256)(128)(2,1)S(1)} %mul.123, bf16[1,16,2048]{2,1,0:T(8,128)(2,1)S(1)} %copy-done.4, bf16[1,16,2048]{2,1,0:T(8,128)(2,1)S(1)} %copy-done.3), kind=kOutput, calls=%fused_computation.22 | convolution fusion | flops 9230336 | bytes 722176 | tf_op jit(solution)/shard_map/dot_general | solution.py:168
  (28 shorter events, 0.4 us)
Async XLA Ops:
  7.2 90.5 %copy-start = (bf16[1,2048,2,384]{3,2,1,0:T(2,128)(2,1)S(1)}, bf16[1,2048,2,384]{3,2,1,0:T(2,128)(2,1)}, u32[]{:S(2)}) copy-start(bf16[1,2048,2,384]{3,2,1,0:T(2,128)(2,1)} %param.18) | copy-start | bytes 9437188
  7.2 68.3 %reduce-scatter.2.cloned.1.call-start = ((), (), s32[]{:S(2)}) async-start(), calls=%async_computation.3 | async-start | bytes 327680 | tf_op jit(solution)/shard_map/reduce_scatter | solution.py:113
  8.4 10.2 %collective-permute-start = (bf16[1,576,2,128]{3,1,2,0:T(8,128)(2,1)S(1)}, bf16[1,576,2,128]{3,1,2,0:T(8,128)(2,1)}, u32[]{:S(2)}, u32[]{:S(2)}) collective-permute-start(bf16[1,576,2,128]{3,1,2,0:T(8,128)(2,1)S(1)} %copy.66), channel_id=1, source_target_pairs={{0,4},{4,0},{8,12},{12,8},{1,5},{5,1},{9,13},{13,9},{2,6},{6,2},{1... | collective-permute-start | bytes 884744 | tf_op jit(solution)/shard_map/ppermute | solution.py:91
  14.8 33.5 %copy-start.5 = (bf16[8,8,8,128]{3,2,1,0:T(8,128)(2,1)S(1)}, bf16[8,8,8,128]{3,2,1,0:T(8,128)(2,1)}, u32[]{:S(2)}) copy-start(bf16[8,8,8,128]{3,2,1,0:T(8,128)(2,1)} %copy.53) | copy-start | bytes 393220
  19.8 28.1 %collective-permute-start.1 = (bf16[1,1152,2,128]{3,1,2,0:T(8,128)(2,1)S(1)}, bf16[1,1152,2,128]{3,1,2,0:T(8,128)(2,1)S(1)}, u32[]{:S(2)}, u32[]{:S(2)}) collective-permute-start(bf16[1,1152,2,128]{3,1,2,0:T(8,128)(2,1)S(1)} %maximum_select_fusion.2), channel_id=1, source_target_pairs={{0,8},{4,12},{8,0},{12,4},{1,9},{5,13},{9,1},{13,5},{2,10},{6,14},... | collective-permute-start | bytes 1769480 | tf_op jit(solution)/shard_map/ppermute | solution.py:91
  50.4 2.2 %copy-start.1 = (bf16[1024,2048]{1,0:T(8,128)(2,1)S(1)}, bf16[1024,2048]{1,0:T(8,128)(2,1)}, u32[]{:S(2)}) copy-start(bf16[1024,2048]{1,0:T(8,128)(2,1)} %param.14) | copy-start | bytes 12582916
  52.6 22.8 %copy-start.3 = (bf16[1,16,2048]{2,1,0:T(8,128)(2,1)S(1)}, bf16[1,16,2048]{2,1,0:T(8,128)(2,1)}, u32[]{:S(2)}) copy-start(bf16[1,16,2048]{2,1,0:T(8,128)(2,1)} %param.13) | copy-start | bytes 196612
  52.6 23.8 %copy-start.7 = (f32[2048]{0:T(1024)S(1)}, f32[2048]{0:T(1024)}, u32[]{:S(2)}) copy-start(f32[2048]{0:T(1024)} %param.15) | copy-start | bytes 24580
  97.7 1.4 %copy-start.2 = (bf16[1,384,2048]{2,1,0:T(8,128)(2,1)S(1)}, bf16[1,384,2048]{2,1,0:T(8,128)(2,1)}, u32[]{:S(2)}) copy-start(bf16[1,384,2048]{2,1,0:T(8,128)(2,1)} %param.19) | copy-start | bytes 4718596
  99.1 5.5 %copy-start.6 = (f32[1,16,8]{1,2,0:T(8,128)S(1)}, f32[1,16,8]{1,2,0:T(8,128)}, u32[]{:S(2)}) copy-start(f32[1,16,8]{1,2,0:T(8,128)} %param.17) | copy-start | bytes 1540
  99.1 19.8 %copy-start.4 = (bf16[1,16,2048]{2,1,0:T(8,128)(2,1)S(1)}, bf16[1,16,2048]{2,1,0:T(8,128)(2,1)}, u32[]{:S(2)}) copy-start(bf16[1,16,2048]{2,1,0:T(8,128)(2,1)} %reduce-scatter.2.cloned.1.call-done) | copy-start | bytes 196612
  100.4 18.5 %all-to-all-start.1 = ((bf16[16,8,2048]{2,1,0:T(8,128)(2,1)}), bf16[16,8,2048]{2,1,0:T(8,128)(2,1)}, u32[]{:S(2)}, u32[]{:S(2)}) async-start(bf16[16,8,2048]{2,1,0:T(8,128)(2,1)} %fusion.12), calls=%async_computation.2 | async-start | bytes 1048576 | tf_op jit(solution)/shard_map/all_to_all | solution.py:165
Sparse Core Ops, SparseCore 0:
  54.3 21.0 reduce-scatter.1
